TPU v7x, 256 devices: a whole 4x4x8 slice. The times are simulated.
256 devices in a mesh: lang: 4 (over x_hi, core), blk: 64 (over x_lo, z, y).
Axes of the slice: x: 4 (x_hi: 2, x_lo: 2; x = x_hi * 2 + x_lo), y: 4, z: 8, core: 2. Of those that a mesh axis runs over, the one named last changes fastest.
Arguments:
- fisher: bfloat16 [8, 4096, 16384], P('lang', None, 'blk'), may hold values from 0.049804688 to 5
- factor_left: bfloat16 [8, 4096, 64], P('lang', 'blk'), may hold values from -6 to 6
- factor_right: bfloat16 [8, 64, 16384], P('lang', None, 'blk'), may hold values from -0.75 to 0.75
- base_weight: bfloat16 [4096, 16384], P(('lang', 'blk')), may hold values from -3 to 3
Outputs:
- merged: bfloat16 [4096, 16384], P(('lang', 'blk'))
All inputs are finite; a program needn't handle non-finite values.
Results may differ from a plain program's by a relative error of at most 0.0011.
Values may be sent and summed in bfloat16 or wider, within the bound.
A program may use at most 128 MiB of HBM per device.

v0:
```python
import jax
import jax.numpy as jnp
from jax import lax
from jax.sharding import PartitionSpec as P


def weighted_sums(fisher_part, change):
    weight_wide = fisher_part.astype(jnp.float32)
    return (jnp.sum(weight_wide * change, axis=0), jnp.sum(weight_wide, axis=0))


def shards(fisher, factor_left, factor_right, base_weight):
    lang_count = lax.axis_size("lang")
    blk_count = lax.axis_size("blk")
    local_langs, full_rows, columns = fisher.shape
    row_count = base_weight.shape[0]
    change = jnp.einsum(
        "lir,lrc->lic",
        lax.all_gather(factor_left, "blk", axis=1, tiled=True),
        factor_right,
        preferred_element_type=jnp.float32,
    )
    weighted, totals = weighted_sums(fisher, change)
    weighted = weighted.reshape(lang_count, blk_count, row_count, columns)
    totals = totals.reshape(lang_count, blk_count, row_count, columns)
    moved = (
        lax.all_to_all(weighted, "blk", split_axis=1, concat_axis=3, tiled=True),
        lax.all_to_all(totals, "blk", split_axis=1, concat_axis=3, tiled=True),
    )
    weighted, totals = (
        lax.psum_scatter(moved[0], "lang", scatter_dimension=0, tiled=True),
        lax.psum_scatter(moved[1], "lang", scatter_dimension=0, tiled=True),
    )
    weighted = weighted.reshape(row_count, columns * blk_count)
    totals = totals.reshape(row_count, columns * blk_count)
    return (base_weight.astype(jnp.float32) + weighted / totals).astype(jnp.bfloat16)


def solution(mesh):
    placed = (
        P("lang", None, "blk"),
        P("lang", "blk", None),
        P("lang", None, "blk"),
        P(("lang", "blk"), None),
    )
    return jax.shard_map(
        shards, mesh=mesh, in_specs=placed, out_specs=P(("lang", "blk"), None), check_vma=False
    )
```

profile of v0, /device:TPU:1, one launch (start us, length us, event | category | flops | bytes accessed | tf_op | source)
XLA Modules:
  0.0 475.5 jit_solution(10156410915796598512)
XLA Ops:
  7.4 0.0 copy-start
  7.4 3.5 convert_reduce_fusion
  10.9 2.4 copy.9
  13.3 13.8 %all-to-all-start.1 = ((f32[4,64,16,256]{3,2,0,1:T(8,128)}), f32[4,64,16,256]{3,2,0,1:T(8,128)}, u32[]{:S(2)}, u32[]{:S(2)}) async-start(f32[4,64,16,256]{3,2,0,1:T(8,128)} %copy.9), calls=%async_computation.2 | async-start | bytes 8388608 | tf_op jit(solution)/shard_map/all_to_all | solution.py:28
  27.1 0.0 all-gather.2.cloned.1.call-start
  27.2 0.7 all-gather.2.cloned.1.call-update
  27.9 0.0 reduce-scatter.5.cloned.1.call-start
  27.9 91.7 %all-to-all-done.1 = f32[4,64,16,256]{3,2,0,1:T(8,128)} async-done(((f32[4,64,16,256]{3,2,0,1:T(8,128)}), f32[4,64,16,256]{3,2,0,1:T(8,128)}, u32[]{:S(2)}, u32[]{:S(2)}) %all-to-all-start.1) | async-done | bytes 4194336 | tf_op jit(solution)/shard_map/all_to_all | solution.py:28
  119.6 4.5 copy.12
  124.2 0.0 reduce-scatter.5.cloned.1.call-update
  124.2 0.0 reduce-scatter.3.cloned.1.call-start
  124.3 178.3 %all-gather.2.cloned.1.call-done = bf16[2,4096,64]{2,1,0:T(8,128)(2,1)} async-done(((bf16[2,64,64]{2,1,0:T(8,128)(2,1)}), bf16[2,4096,64]{2,1,0:T(8,128)(2,1)}) %all-gather.2.cloned.1.call-update) | async-done | bytes 1048592 | tf_op jit(solution)/shard_map/all_gather | solution.py:19
  302.6 0.0 copy-done
  302.6 4.4 fusion
  307.0 0.5 copy.7
  307.5 61.9 %all_to_all.36 = f32[4,64,16,256]{3,2,0,1:T(8,128)S(1)} all-to-all(f32[4,64,16,256]{3,2,0,1:T(8,128)S(1)} %copy.7), channel_id=1, replica_groups=mesh['lang'=4,'blk'=64] {'blk'}, dimensions={1} | all-to-all | bytes 8388608 | tf_op jit(solution)/shard_map/all_to_all | solution.py:27
  369.4 2.4 copy.11
  371.8 0.0 copy-start.1
  371.8 0.0 reduce-scatter.3.cloned.1.call-update
  371.8 0.0 reduce-scatter.5.cloned.1.call-done
  371.8 93.8 %reduce-scatter.3.cloned.1.call-done = f32[1,1,16,16384]{3,2,0,1:T(8,128)} async-done(((f32[4,1,16,16384]{3,2,0,1:T(8,128)}), f32[1,1,16,16384]{3,2,0,1:T(8,128)}) %reduce-scatter.3.cloned.1.call-update) | async-done | bytes 1048592 | tf_op jit(solution)/shard_map/reduce_scatter | solution.py:31
  465.6 0.0 copy-done.1
  465.6 2.5 fusion.1
Async XLA Ops:
  7.4 295.2 %copy-start = (bf16[2,64,256]{2,1,0:T(8,128)(2,1)S(1)}, bf16[2,64,256]{2,1,0:T(8,128)(2,1)}, u32[]{:S(2)}) copy-start(bf16[2,64,256]{2,1,0:T(8,128)(2,1)} %param.6) | copy-start | bytes 196612
  13.3 106.4 %all-to-all-start.1 = ((f32[4,64,16,256]{3,2,0,1:T(8,128)}), f32[4,64,16,256]{3,2,0,1:T(8,128)}, u32[]{:S(2)}, u32[]{:S(2)}) async-start(f32[4,64,16,256]{3,2,0,1:T(8,128)} %copy.9), calls=%async_computation.2 | async-start | bytes 8388608 | tf_op jit(solution)/shard_map/all_to_all | solution.py:28
  27.1 275.4 %all-gather.2.cloned.1.call-start = ((), (), s32[]{:S(2)}) async-start(), calls=%async_computation.4 | async-start | bytes 2129920 | tf_op jit(solution)/shard_map/all_gather | solution.py:19
  27.9 343.9 %reduce-scatter.5.cloned.1.call-start = ((), (), s32[]{:S(2)}) async-start(), calls=%async_computation.6 | async-start | bytes 5242880 | tf_op jit(solution)/shard_map/reduce_scatter | solution.py:32
  124.2 341.4 %reduce-scatter.3.cloned.1.call-start = ((), (), s32[]{:S(2)}) async-start(), calls=%async_computation.5 | async-start | bytes 5242880 | tf_op jit(solution)/shard_map/reduce_scatter | solution.py:31
  371.8 93.8 %copy-start.1 = (bf16[16,16384]{1,0:T(8,128)(2,1)S(1)}, bf16[16,16384]{1,0:T(8,128)(2,1)}, u32[]{:S(2)}) copy-start(bf16[16,16384]{1,0:T(8,128)(2,1)} %param.7) | copy-start | bytes 1572868
Sparse Core Ops, SparseCore 0:
  29.9 272.6 all-gather.1
Sparse Core Ops, SparseCore 1:
  124.3 63.0 reduce-scatter.4
  371.9 93.7 reduce-scatter.2
where the time goes:
time: 476 us
  waiting for transfers between devices  365 us (77%)
  blocking collectives  61.9 us (13%)
  between operations  14.9 us (3%)
  starting transfers between devices  14 us (3%)
  local copies, waits for them, and re-layouts  9.77 us (2%)
  other arithmetic  6 us (1%)
    all_gather x1, waiting for transfers between devices, shards(): lax.all_gather(factor_left, 'blk', axis=1, tiled=True)  178 us
    reduce_scatter x1, waiting for transfers between devices, shards(): lax.psum_scatter(moved[0], 'lang', scatter_dimension=0, tiled=True)  93.8 us
    all_to_all x1, waiting for transfers between devices, shards(): lax.all_to_all(totals, 'blk', split_axis=1, concat_axis=3, tiled=True)  91.7 us
    all_to_all x1, blocking collectives, shards(): lax.all_to_all(weighted, 'blk', split_axis=1, concat_axis=3, tiled=True)  61.9 us
    all_to_all x1, starting transfers between devices, shards(): lax.all_to_all(totals, 'blk', split_axis=1, concat_axis=3, tiled=True)  13.8 us
  transfers between devices with their start and end apart: 4, of which 3 were waited for; matrix products, arithmetic and copies ran while one was open for 2% of the time, Pallas kernels for 0%

commit v1 on v0

--- a/solution.py
+++ b/solution.py
@@ -2,6 +2,13 @@
 import jax.numpy as jnp
 from jax import lax
 from jax.sharding import PartitionSpec as P
+
+
+def trade_parts(x, mesh_axis, split, join):
+    size = lax.axis_size(mesh_axis)
+    blocks = jnp.stack(jnp.split(x, size, axis=split), axis=0)
+    blocks = lax.all_to_all(blocks, mesh_axis, split_axis=0, concat_axis=0)
+    return jnp.concatenate(blocks, axis=join)
 
 
 def weighted_sums(fisher_part, change):
@@ -24,7 +31,7 @@
     weighted = weighted.reshape(lang_count, blk_count, row_count, columns)
     totals = totals.reshape(lang_count, blk_count, row_count, columns)
     moved = (
-        lax.all_to_all(weighted, "blk", split_axis=1, concat_axis=3, tiled=True),
+        trade_parts(weighted, "blk", 1, 3),
         lax.all_to_all(totals, "blk", split_axis=1, concat_axis=3, tiled=True),
     )
     weighted, totals = (

time: 476 us -> 512 us (1.076)
  local copies, waits for them, and re-layouts: 9.77 us -> 51.1 us
  waiting for transfers between devices: 365 us -> 354 us
  blocking collectives: 61.9 us -> 67.3 us
    all_to_all x1, waiting for transfers between devices: 91.7 us -> 0.01 us  [shards(): lax.all_to_all(totals, 'blk', split_axis=1, concat_axis=3, tiled=True)]
    all_gather x1, waiting for transfers between devices: 178 us -> 260 us  [shards(): lax.all_gather(factor_left, 'blk', axis=1, tiled=True)]
    unnamed x4 -> x69, local copies, waits for them, and re-layouts: 0.01 us -> 40.3 us
    reduce_scatter x1, waiting for transfers between devices: 93.8 us -> 58 us  [shards(): lax.psum_scatter(moved[0], 'lang', scatter_dimension=0, tiled=True)]
    reduce_scatter x1, waiting for transfers between devices: 0.03 us -> 35 us  [shards(): lax.psum_scatter(moved[1], 'lang', scatter_dimension=0, tiled=True)]
    all_to_all x1, blocking collectives: 61.9 us -> 67.3 us  [trade_parts(): blocks = lax.all_to_all(blocks, mesh_axis, split_axis=0, concat_axis=0)]
  transfers between devices with their start and end apart: 4 -> 4, of which waited for: 3 -> 3; matrix products, arithmetic and copies ran while one was open for 2% -> 11% of each run, Pallas kernels for 0% -> 0%
where the time goes in v1:
time: 512 us
  waiting for transfers between devices  354 us (69%)
  blocking collectives  67.3 us (13%)
  local copies, waits for them, and re-layouts  51.1 us (10%)
  between operations  14.9 us (3%)
  starting transfers between devices  13.9 us (3%)
  other arithmetic  6 us (1%)
    all_gather x1, waiting for transfers between devices, shards(): lax.all_gather(factor_left, 'blk', axis=1, tiled=True)  260 us
    all_to_all x1, blocking collectives, trade_parts(): blocks = lax.all_to_all(blocks, mesh_axis, split_axis=0, concat_axis=0)  67.3 us
    reduce_scatter x1, waiting for transfers between devices, shards(): lax.psum_scatter(moved[0], 'lang', scatter_dimension=0, tiled=True)  58 us
    unnamed x69, local copies, waits for them, and re-layouts  40.3 us
    reduce_scatter x1, waiting for transfers between devices, shards(): lax.psum_scatter(moved[1], 'lang', scatter_dimension=0, tiled=True)  35 us
    all_to_all x1, starting transfers between devices, shards(): lax.all_to_all(totals, 'blk', split_axis=1, concat_axis=3, tiled=True)  13.8 us
  transfers between devices with their start and end apart: 4, of which 3 were waited for; matrix products, arithmetic and copies ran while one was open for 11% of the time, Pallas kernels for 0%

profile of v1, /device:TPU:1, one launch (start us, length us, event | category | flops | bytes accessed | tf_op | source)
XLA Modules:
  0.0 511.6 jit_solution(11531673330368168451)
XLA Ops:
  7.4 0.7 all-gather.2.cloned.1.call-update
  8.1 3.5 convert_reduce_fusion
  11.6 2.4 copy.260
  14.0 13.8 %all-to-all-start.1 = ((f32[4,64,16,256]{3,2,0,1:T(8,128)}), f32[4,64,16,256]{3,2,0,1:T(8,128)}, u32[]{:S(2)}, u32[]{:S(2)}) async-start(f32[4,64,16,256]{3,2,0,1:T(8,128)} %copy.260), calls=%async_computation.2 | async-start | bytes 8388608 | tf_op jit(solution)/shard_map/all_to_all | solution.py:35
  27.9 260.2 %all-gather.2.cloned.1.call-done = bf16[2,4096,64]{2,1,0:T(8,128)(2,1)} async-done(((bf16[2,64,64]{2,1,0:T(8,128)(2,1)}), bf16[2,4096,64]{2,1,0:T(8,128)(2,1)}) %all-gather.2.cloned.1.call-update) | async-done | bytes 1048592 | tf_op jit(solution)/shard_map/all_gather | solution.py:26
  288.1 4.4 fusion
  292.5 0.7 constant_dynamic-update-slice_fusion.63
  293.2 1.1 constant_dynamic-update-slice_fusion.62
  295.0 0.6 constant_dynamic-update-slice_fusion.60
  300.7 0.6 constant_dynamic-update-slice_fusion.51
  301.9 0.6 constant_dynamic-update-slice_fusion.49
  307.6 0.6 constant_dynamic-update-slice_fusion.40
  310.2 0.6 constant_dynamic-update-slice_fusion.36
  315.2 0.6 constant_dynamic-update-slice_fusion.28
  318.4 0.6 constant_dynamic-update-slice_fusion.23
  321.5 0.6 constant_dynamic-update-slice_fusion.18
  332.2 0.6 constant_dynamic-update-slice_fusion.1
  332.9 4.6 copy.326
  337.5 1.5 constant_dynamic-update-slice_fusion
  339.0 67.3 %all_to_all.23 = f32[64,4,1,16,256]{4,3,1,2,0:T(8,128)S(1)} all-to-all(f32[64,4,1,16,256]{4,3,1,2,0:T(8,128)} %constant_dynamic-update-slice_fusion), channel_id=1, replica_groups=mesh['lang'=4,'blk'=64] {'blk'}, dimensions={0} | all-to-all | bytes 8388608 | tf_op jit(solution)/shard_map/all_to_all | solution.py:10
  406.2 2.3 copy.325
  408.6 35.0 %reduce-scatter.5.cloned.1.call-done = f32[1,1,16,16384]{3,2,0,1:T(8,128)} async-done(((f32[4,1,16,16384]{3,2,0,1:T(8,128)}), f32[1,1,16,16384]{3,2,0,1:T(8,128)}) %reduce-scatter.5.cloned.1.call-update) | async-done | bytes 1048592 | tf_op jit(solution)/shard_map/reduce_scatter | solution.py:39
  443.6 58.0 %reduce-scatter.3.cloned.1.call-done = f32[1,1,16,16384]{3,2,0,1:T(8,128)} async-done(((f32[4,1,16,16384]{3,2,0,1:T(8,128)}), f32[1,1,16,16384]{3,2,0,1:T(8,128)}) %reduce-scatter.3.cloned.1.call-update) | async-done | bytes 1048592 | tf_op jit(solution)/shard_map/reduce_scatter | solution.py:38
  501.6 2.5 fusion.1
  (64 shorter events, 32.9 us)
Async XLA Ops:
  7.4 280.7 %copy-start = (bf16[2,64,256]{2,1,0:T(8,128)(2,1)S(1)}, bf16[2,64,256]{2,1,0:T(8,128)(2,1)}, u32[]{:S(2)}) copy-start(bf16[2,64,256]{2,1,0:T(8,128)(2,1)} %param.6) | copy-start | bytes 196612
  7.4 280.7 %all-gather.2.cloned.1.call-start = ((), (), s32[]{:S(2)}) async-start(), calls=%async_computation.4 | async-start | bytes 2129920 | tf_op jit(solution)/shard_map/all_gather | solution.py:26
  14.0 318.9 %all-to-all-start.1 = ((f32[4,64,16,256]{3,2,0,1:T(8,128)}), f32[4,64,16,256]{3,2,0,1:T(8,128)}, u32[]{:S(2)}, u32[]{:S(2)}) async-start(f32[4,64,16,256]{3,2,0,1:T(8,128)} %copy.260), calls=%async_computation.2 | async-start | bytes 8388608 | tf_op jit(solution)/shard_map/all_to_all | solution.py:35
  27.9 415.7 %reduce-scatter.5.cloned.1.call-start = ((), (), s32[]{:S(2)}) async-start(), calls=%async_computation.6 | async-start | bytes 5242880 | tf_op jit(solution)/shard_map/reduce_scatter | solution.py:39
  292.5 39.7 %copy-start.1 = (f32[4096,256]{1,0:T(8,128)}, f32[4096,256]{1,0:T(8,128)S(1)}, u32[]{:S(2)}) copy-start(f32[4096,256]{1,0:T(8,128)S(1)} %fusion) | copy-start | bytes 12582916
  337.5 164.2 %reduce-scatter.3.cloned.1.call-start = ((), (), s32[]{:S(2)}) async-start(), calls=%async_computation.5 | async-start | bytes 5242880 | tf_op jit(solution)/shard_map/reduce_scatter | solution.py:38
  408.6 93.1 %copy-start.2 = (bf16[16,16384]{1,0:T(8,128)(2,1)S(1)}, bf16[16,16384]{1,0:T(8,128)(2,1)}, u32[]{:S(2)}) copy-start(bf16[16,16384]{1,0:T(8,128)(2,1)} %param.7) | copy-start | bytes 1572868
Sparse Core Ops, SparseCore 0:
  10.1 277.9 all-gather.1
Sparse Core Ops, SparseCore 1:
  337.5 106.0 reduce-scatter.4
  446.5 55.1 reduce-scatter.2
